TPU v7x, 32 devices: a whole 2x2x4 slice. The times are simulated.
32 devices in a mesh: wide: 8 (over z, y), narrow: 4 (over x, core).
Axes of the slice: x: 2, y: 2, z: 4, core: 2. Of those that a mesh axis runs over, the one named last changes fastest.
Arguments:
- entry_factor: bfloat16 [288, 4, 64, 1024], P('wide', 'narrow'), may hold values from -6 to 6
- entry_panel: int32 [288, 4], P('wide', 'narrow'), may hold values from 0 to 1
- entry_target: int32 [288, 4], P('wide', 'narrow'), may hold values from 0 to 7, as said below
- entry_count: int32 [4, 8], P('narrow', 'wide'), may hold values from 1 to 36, 96 in all within a row
- panel_shared: bfloat16 [16, 64, 1024], P('wide', None, 'narrow'), may hold values from -0.1875 to 0.1875
- coupling: float32 [16, 64, 64], P('wide'), may hold values from -0.75 to 0.75
- probes: bfloat16 [32, 64, 1024], P('narrow'), may hold values from -6 to 6
Outputs:
- left_factor: float32 [32, 64, 1024], P('narrow', None, 'wide')
- right_factor: float32 [32, 64, 1024], P('narrow', None, 'wide')
Inputs may be any that keep to these rules, and one draw needn't show every extreme that they name: `entry_panel`: the local panel of an entry of any slot, live or not. `entry_target`: the local target of an entry; every target has at least one live entry. `entry_count`: the live slots of one device; for every owner the counts over the 8 wide indices sum to 96, and some device holds exactly 36.
All inputs are finite; a program needn't handle non-finite values.
Results may differ from a plain program's by a relative error of at most 0.0036.
Values may be sent and summed in bfloat16 or wider, within the bound.
A program may use at most 64 MiB of HBM per device.

v0:
```python
import math
import jax
import jax.numpy as jnp
from jax import lax
from jax.sharding import PartitionSpec as P


def shards(entry_factor, entry_panel, entry_target, entry_count, panel_shared, coupling, probes):
    highest = lax.Precision.HIGHEST
    factors = entry_factor[:, 0]
    slot_count = factors.shape[0]
    rank_dim = factors.shape[1]
    full_width = factors.shape[2]
    panel_count = panel_shared.shape[0]
    target_count = probes.shape[0]
    live_mask = (jnp.arange(slot_count) < entry_count[0, 0]).astype(jnp.float32)
    pick_panel = (entry_panel == jnp.arange(panel_count)[None, :]).astype(jnp.float32) * live_mask[
        :, None
    ]
    pick_target = (entry_target == jnp.arange(target_count)[None, :]).astype(jnp.float32)
    pair_pick = (pick_panel[:, :, None] * pick_target[:, None, :]).reshape(
        slot_count, panel_count * target_count
    )
    gathered = lax.all_gather(panel_shared, "narrow", axis=2, tiled=True)
    projected = jnp.einsum("drb,tkb->dtrk", gathered, probes, preferred_element_type=jnp.float32)
    coefficients = jnp.einsum("dij,dtjk->dtik", coupling, projected, precision=highest).astype(
        jnp.bfloat16
    )
    coeff_table = coefficients.reshape(panel_count * target_count, rank_dim * rank_dim)
    chosen = jnp.dot(
        pair_pick.astype(jnp.bfloat16), coeff_table, preferred_element_type=jnp.float32
    )
    chosen = chosen.astype(jnp.bfloat16).reshape(slot_count, rank_dim, rank_dim)
    contributions = jnp.einsum("eji,ejb->eib", chosen, factors, preferred_element_type=jnp.float32)
    sketch = jnp.einsum("et,eib->tib", pick_target, contributions, precision=highest)
    wide_count = lax.axis_size("wide")
    share_cols = full_width // wide_count
    sketch_sum = lax.psum(sketch, "wide")
    gram_matrix = jnp.einsum("tib,tjb->tij", sketch_sum, sketch_sum, precision=highest)
    lower_factor = jnp.linalg.cholesky(gram_matrix)
    basis = jax.scipy.linalg.solve_triangular(lower_factor, sketch_sum, lower=True)
    basis_round = basis.astype(jnp.bfloat16)
    own_basis = lax.dynamic_slice_in_dim(basis, lax.axis_index("wide") * share_cols, share_cols, 2)
    selected = jnp.einsum(
        "et,tkb->ekb",
        pick_target.astype(jnp.bfloat16),
        basis_round,
        preferred_element_type=jnp.float32,
    )
    selected = selected.astype(jnp.bfloat16)
    back_terms = jnp.einsum("eib,ekb->eik", factors, selected, preferred_element_type=jnp.float32)
    summed = jnp.einsum("ep,eik->pik", pair_pick, back_terms, precision=highest)
    summed = summed.reshape(panel_count, target_count, rank_dim, rank_dim)
    middle_terms = jnp.einsum("dtik,dij->dtkj", summed, coupling, precision=highest)
    partial_rows = jnp.einsum(
        "dtkj,djb->tkb", middle_terms, gathered.astype(jnp.float32), precision=highest
    )
    coeff_part = lax.psum_scatter(partial_rows, "wide", scatter_dimension=2, tiled=True)
    root_width = math.sqrt(full_width)
    return (own_basis * root_width, coeff_part / root_width)


def solution(mesh):
    placed = (
        P("wide", "narrow", None, None),
        P("wide", "narrow"),
        P("wide", "narrow"),
        P("narrow", "wide"),
        P("wide", None, "narrow"),
        P("wide", None, None),
        P("narrow", None, None),
    )
    return jax.shard_map(
        shards,
        mesh=mesh,
        in_specs=placed,
        out_specs=(P("narrow", None, "wide"), P("narrow", None, "wide")),
        check_vma=False,
    )
```

profile of v0, /device:TPU:0, one launch (start us, length us, event | category | flops | bytes accessed | tf_op | source)
XLA Modules:
  0.0 328.4 jit_solution(10725598671400621314)
XLA Ops:
  7.2 0.0 copy-start
  7.2 0.0 copy-start.4
  7.2 0.0 copy-start.6
  7.2 0.0 all-reduce.2.cloned.1.call-start
  7.2 0.7 fusion.36
  8.0 7.4 %all_gather.3 = bf16[2,64,1024]{2,1,0:T(8,128)(2,1)S(1)} all-gather(bf16[2,64,256]{2,1,0:T(8,128)(2,1)} %param.11), channel_id=1, replica_groups=mesh['wide'=8,'narrow'=4] {'narrow'}, dimensions={2}, use_global_device_ids=true | all-gather | bytes 327680 | tf_op jit(solution)/shard_map/all_gather | solution.py:24
  15.4 0.0 copy-done
  15.4 0.0 copy-start.2
  15.4 0.5 convolution_bitcast_fusion.1
  15.9 0.2 copy-done.2
  16.1 0.0 copy-done.4
  16.1 0.6 fusion.18
  16.7 0.2 copy.21
  16.9 0.3 reshape.98
  17.8 0.0 copy-done.6
  17.9 0.3 convolution_convert_fusion
  18.1 0.6 reshape.99
  18.8 0.0 copy-start.5
  18.8 3.8 %fusion.4 = f32[36,64,1024]{2,1,0:T(8,128)S(1)} fusion(bf16[36,64,64]{2,1,0:T(8,128)(2,1)S(1)} %reshape.99, bf16[36,1,64,1024]{3,2,1,0:T(8,128)(2,1)} %param.7), kind=kOutput, calls=%fused_computation.4 | convolution fusion | flops 301989888 | bytes 14450688 | tf_op jit(solution)/shard_map/eji,ejb->eib/dot_general | solution.py:34
  22.6 0.0 copy-done.5
  22.6 10.1 %fusion = f32[8,64,1024]{2,0,1:T(8,128)} fusion(f32[36,64,1024]{2,1,0:T(8,128)S(1)} %fusion.4, s32[36]{0:T(128)S(1)} %bitcast.78), kind=kOutput, calls=%fused_computation | convolution fusion | flops 226492704 | bytes 11534480 | tf_op jit(solution)/shard_map/et,eib->tib/dot_general | solution.py:35
  32.7 0.0 all-reduce.2.cloned.1.call-update
  32.7 0.0 reduce-scatter.2.cloned.1.call-start
  32.8 103.7 %all-reduce.2.cloned.1.call-done = f32[8,64,1024]{2,0,1:T(8,128)} async-done(((f32[8,64,1024]{2,0,1:T(8,128)}), f32[8,64,1024]{2,0,1:T(8,128)}) %all-reduce.2.cloned.1.call-update) | async-done | bytes 2097168 | tf_op jit(solution)/shard_map/psum | solution.py:38
  136.4 0.0 copy-start.1
  136.4 6.7 %fusion.9 = f32[8,64,64]{2,1,0:T(8,128)S(1)} fusion(f32[8,64,1024]{2,0,1:T(8,128)} %all-reduce.2.cloned.1.call-done), kind=kOutput, calls=%fused_computation.11 | convolution fusion | flops 402653184 | bytes 2228224 | tf_op jit(solution)/shard_map/tib,tjb->tij/dot_general | solution.py:39
  143.1 0.8 copy.26
  144.0 1.7 fusion.25
  145.7 47.6 %custom-call.8 = f32[8,64,64]{2,1,0:T(8,128)S(1)} custom-call(f32[8,64,64]{2,1,0:T(8,128)} %fusion.25), custom_call_target="Cholesky" | custom-call | tf_op jit(solution)/shard_map/jit(cholesky)/cholesky | solution.py:40
  193.3 0.1 compare_reduce_fusion
  193.4 0.8 select_bitcast_fusion
  194.3 40.3 %custom-call.9 = f32[8,1,64,64]{2,3,1,0:T(8,128)S(1)} custom-call(f32[8,1,64,64]{3,2,1,0:T(8,128)} %select_bitcast_fusion), custom_call_target="InvertDiagBlocksLowerTriangular" | custom-call | tf_op jit(solution)/shard_map/jit(_solve_triangular)/vmap()/triangular_solve | solution.py:41
  234.5 0.0 copy-done.1
  234.5 4.4 %fusion.42 = (bf16[8,64,1024]{2,1,0:T(8,128)(2,1)S(1)}, f32[8,64,1024]{2,1,0:T(8,128)}) fusion(f32[8,64,1024]{2,0,1:T(8,128)S(1)} %copy-done.1, f32[8,1,64,64]{2,3,1,0:T(8,128)S(1)} %custom-call.9), kind=kOutput, calls=%fused_computation.53 | convolution fusion | flops 403177472 | bytes 5373952 | tf_op jit(solution)/shard_map/jit(_solve_triangular)/vmap()/triangular_solve | solution.py:41
  238.9 1.6 convolution_convert_fusion.1
  240.5 5.5 %fusion.11 = f32[36,64,64]{1,2,0:T(8,128)S(1)} fusion(bf16[36,1,64,1024]{3,2,1,0:T(8,128)(2,1)} %param.7, bf16[36,64,1024]{2,0,1:T(8,128)(2,1)S(1)} %convolution_convert_fusion.1), kind=kOutput, calls=%fused_computation.14 | convolution fusion | flops 301989888 | bytes 10027008 | tf_op jit(solution)/shard_map/eib,ekb->eik/dot_general | solution.py:51
  246.0 0.5 copy.31
  246.5 0.0 copy-start.3
  246.5 0.8 fusion.16
  247.3 1.8 fusion.21
  249.1 0.0 copy-done.3
  249.1 2.3 convolution_bitcast_fusion
  251.4 0.0 reduce-scatter.2.cloned.1.call-update
  251.5 1.7 dynamic-slice_multiply_fusion
  253.1 66.7 %reduce-scatter.2.cloned.1.call-done = f32[8,64,128]{2,1,0:T(8,128)} async-done(((f32[8,64,1024]{2,1,0:T(8,128)}), f32[8,64,128]{2,1,0:T(8,128)}) %reduce-scatter.2.cloned.1.call-update) | async-done | bytes 262160 | tf_op jit(solution)/shard_map/reduce_scatter | solution.py:58
  319.8 1.7 broadcast_multiply_fusion
  (5 shorter events, 0.1 us)
Async XLA Ops:
  7.2 8.2 %copy-start = (bf16[8,64,1024]{2,1,0:T(8,128)(2,1)S(1)}, bf16[8,64,1024]{2,1,0:T(8,128)(2,1)}, u32[]{:S(2)}) copy-start(bf16[8,64,1024]{2,1,0:T(8,128)(2,1)} %param.13) | copy-start | bytes 3145732
  7.2 8.9 %copy-start.4 = (f32[2,64,64]{2,1,0:T(8,128)S(1)}, f32[2,64,64]{2,1,0:T(8,128)}, u32[]{:S(2)}) copy-start(f32[2,64,64]{2,1,0:T(8,128)} %param.12) | copy-start | bytes 98308
  7.2 10.6 %copy-start.6 = (s32[36,1]{0,1:T(1,128)S(1)}, s32[36,1]{0,1:T(1,128)}, u32[]{:S(2)}) copy-start(s32[36,1]{0,1:T(1,128)} %param.8) | copy-start | bytes 436
  7.2 129.2 %all-reduce.2.cloned.1.call-start = ((), (), s32[]{:S(2)}) async-start(), calls=%async_computation.1 | async-start | bytes 4194304 | tf_op jit(solution)/shard_map/psum | solution.py:38
  15.4 0.7 copy-start.2
  18.8 3.8 %copy-start.5 = (s32[36,1]{0,1:T(1,128)S(1)}, s32[36,1]{0,1:T(1,128)}, u32[]{:S(2)}) copy-start(s32[36,1]{0,1:T(1,128)} %param.9) | copy-start | bytes 436
  32.7 287.2 %reduce-scatter.2.cloned.1.call-start = ((), (), s32[]{:S(2)}) async-start(), calls=%async_computation.2 | async-start | bytes 2359296 | tf_op jit(solution)/shard_map/reduce_scatter | solution.py:58
  136.4 98.1 %copy-start.1 = (f32[8,64,1024]{2,0,1:T(8,128)S(1)}, f32[8,64,1024]{2,0,1:T(8,128)}, u32[]{:S(2)}) copy-start(f32[8,64,1024]{2,0,1:T(8,128)} %all-reduce.2.cloned.1.call-done) | copy-start | bytes 6291460
  246.5 2.6 copy-start.3
Sparse Core Ops, SparseCore 0:
  32.8 103.5 all-reduce.1
  251.6 68.2 reduce-scatter.1
where the time goes:
time: 329 us; the launch traced here: 328 us
  waiting for transfers between devices  170 us (52%)
  other arithmetic  94.6 us (29%)
  matrix products  38.3 us (12%)
  between operations  14.9 us (5%)
  blocking collectives  7.42 us (2%)
    psum x1, waiting for transfers between devices, shards(): sketch_sum = lax.psum(sketch, 'wide')  104 us
    reduce_scatter x1, waiting for transfers between devices, shards(): lax.psum_scatter(partial_rows, 'wide', scatter_dimension=2, tiled=True)  66.7 us
    another operation x4, other arithmetic, shards(): lower_factor = jnp.linalg.cholesky(gram_matrix)  47.8 us
    another operation x3, other arithmetic, shards(): jax.scipy.linalg.solve_triangular(lower_factor, sketch_sum, lower=True)  41.1 us
    dot_general x1, matrix products, shards(): jnp.einsum('et,eib->tib', pick_target, contributions, precision=highest)  10.1 us
    all_gather x1, blocking collectives, shards(): gathered = lax.all_gather(panel_shared, 'narrow', axis=2, tiled=True)  7.42 us
    dot_general x1, matrix products, shards(): jnp.einsum('tib,tjb->tij', sketch_sum, sketch_sum, precision=highest)  6.7 us
  transfers between devices with their start and end apart: 2, of which 2 were waited for; matrix products, arithmetic and copies ran while one was open for 1% of the time, Pallas kernels for 0%

commit v1 on v0

--- a/solution.py
+++ b/solution.py
@@ -35,7 +35,8 @@
     sketch = jnp.einsum("et,eib->tib", pick_target, contributions, precision=highest)
     wide_count = lax.axis_size("wide")
     share_cols = full_width // wide_count
-    sketch_sum = lax.psum(sketch, "wide")
+    mid_arr = lax.all_gather(sketch, "wide")
+    sketch_sum = jnp.sum(mid_arr, axis=0)
     gram_matrix = jnp.einsum("tib,tjb->tij", sketch_sum, sketch_sum, precision=highest)
     lower_factor = jnp.linalg.cholesky(gram_matrix)
     basis = jax.scipy.linalg.solve_triangular(lower_factor, sketch_sum, lower=True)

time: 329 us -> 459 us (1.40)
  waiting for transfers between devices: 170 us -> 294 us
  other arithmetic: 94.6 us -> 103 us
    all_gather x0 -> x1, waiting for transfers between devices: none -> 229 us  [shards(): mid_arr = lax.all_gather(sketch, 'wide')]
    psum x1 -> x0, waiting for transfers between devices: 104 us -> none  [shards(): sketch_sum = lax.psum(sketch, 'wide')]
    reduce_sum x0 -> x1, other arithmetic: none -> 8.23 us  [shards(): sketch_sum = jnp.sum(mid_arr, axis=0)]
  transfers between devices with their start and end apart: 2 -> 2, of which waited for: 2 -> 2; matrix products, arithmetic and copies ran while one was open for 1% -> 0% of each run, Pallas kernels for 0% -> 0%
where the time goes in v1:
time: 459 us; the launch traced here: 458 us
  waiting for transfers between devices  294 us (64%)
  other arithmetic  103 us (22%)
  matrix products  36 us (8%)
  between operations  14.9 us (3%)
  blocking collectives  7.42 us (2%)
    all_gather x1, waiting for transfers between devices, shards(): mid_arr = lax.all_gather(sketch, 'wide')  229 us
    reduce_scatter x1, waiting for transfers between devices, shards(): lax.psum_scatter(partial_rows, 'wide', scatter_dimension=2, tiled=True)  65.7 us
    another operation x4, other arithmetic, shards(): lower_factor = jnp.linalg.cholesky(gram_matrix)  47.8 us
    another operation x3, other arithmetic, shards(): jax.scipy.linalg.solve_triangular(lower_factor, sketch_sum, lower=True)  41.1 us
    dot_general x1, matrix products, shards(): jnp.einsum('et,eib->tib', pick_target, contributions, precision=highest)  10.1 us
  transfers between devices with their start and end apart: 2, of which 2 were waited for; matrix products, arithmetic and copies ran while one was open for 0% of the time, Pallas kernels for 0%

profile of v1, /device:TPU:0, one launch (start us, length us, event | category | flops | bytes accessed | tf_op | source)
XLA Modules:
  0.0 458.2 jit_solution(83625696495549002)
XLA Ops:
  7.2 0.0 copy-start
  7.2 0.0 copy-start.3
  7.2 0.0 copy-start.5
  7.2 0.0 all-gather.3.cloned.1.call-start
  7.2 0.7 fusion.36
  8.0 7.4 %all_gather.9 = bf16[2,64,1024]{2,1,0:T(8,128)(2,1)S(1)} all-gather(bf16[2,64,256]{2,1,0:T(8,128)(2,1)} %param.11), channel_id=1, replica_groups=mesh['wide'=8,'narrow'=4] {'narrow'}, dimensions={2}, use_global_device_ids=true | all-gather | bytes 327680 | tf_op jit(solution)/shard_map/all_gather | solution.py:24
  15.4 0.0 copy-done
  15.4 0.0 copy-start.1
  15.4 0.5 convolution_bitcast_fusion.1
  15.9 0.2 copy-done.1
  16.1 0.0 copy-done.3
  16.1 0.6 fusion.18
  16.7 0.2 copy.27
  16.9 0.3 reshape.98
  17.8 0.0 copy-done.5
  17.9 0.3 convolution_convert_fusion
  18.1 0.6 reshape.99
  18.8 0.0 copy-start.4
  18.8 3.8 fusion.4
  22.6 0.0 copy-done.4
  22.6 10.1 %fusion = f32[8,64,1024]{2,0,1:T(8,128)} fusion(f32[36,64,1024]{2,1,0:T(8,128)S(1)} %fusion.4, s32[36]{0:T(128)S(1)} %bitcast.80), kind=kOutput, calls=%fused_computation.1 | convolution fusion | flops 226492704 | bytes 11534480 | tf_op jit(solution)/shard_map/et,eib->tib/dot_general | solution.py:35
  32.7 0.0 all-gather.3.cloned.1.call-update
  32.7 0.0 reduce-scatter.2.cloned.1.call-start
  32.8 228.6 %all-gather.3.cloned.1.call-done = f32[64,64,1024]{2,0,1:T(8,128)} async-done(((f32[8,64,1024]{2,0,1:T(8,128)}), f32[64,64,1024]{2,0,1:T(8,128)}) %all-gather.3.cloned.1.call-update) | async-done | bytes 16777232 | tf_op jit(solution)/shard_map/all_gather | solution.py:38
  261.4 8.2 %bitcast_reduce_fusion = f32[8,64,1024]{2,0,1:T(8,128)S(1)} fusion(f32[64,64,1024]{2,0,1:T(8,128)} %all-gather.3.cloned.1.call-done), kind=kLoop, calls=%fused_computation | loop fusion | flops 3670016 | bytes 18874368 | tf_op jit(solution)/shard_map/reduce_sum | solution.py:39
  269.7 4.4 fusion.9
  274.0 0.8 copy.32
  274.9 1.7 fusion.25
  276.6 47.6 %custom-call.8 = f32[8,64,64]{2,1,0:T(8,128)S(1)} custom-call(f32[8,64,64]{2,1,0:T(8,128)} %fusion.25), custom_call_target="Cholesky" | custom-call | tf_op jit(solution)/shard_map/jit(cholesky)/cholesky | solution.py:41
  324.2 0.1 compare_reduce_fusion
  324.3 0.8 select_bitcast_fusion
  325.2 40.3 %custom-call.9 = f32[8,1,64,64]{2,3,1,0:T(8,128)S(1)} custom-call(f32[8,1,64,64]{3,2,1,0:T(8,128)} %select_bitcast_fusion), custom_call_target="InvertDiagBlocksLowerTriangular" | custom-call | tf_op jit(solution)/shard_map/jit(_solve_triangular)/vmap()/triangular_solve | solution.py:42
  365.4 4.4 fusion.42
  369.8 1.6 convolution_convert_fusion.1
  371.4 5.5 %fusion.11 = f32[36,64,64]{1,2,0:T(8,128)S(1)} fusion(bf16[36,1,64,1024]{3,2,1,0:T(8,128)(2,1)} %param.7, bf16[36,64,1024]{2,0,1:T(8,128)(2,1)S(1)} %convolution_convert_fusion.1), kind=kOutput, calls=%fused_computation.15 | convolution fusion | flops 301989888 | bytes 10027008 | tf_op jit(solution)/shard_map/eib,ekb->eik/dot_general | solution.py:52
  376.9 0.5 copy.37
  377.4 0.0 copy-start.2
  377.4 0.8 fusion.16
  378.1 1.8 fusion.21
  380.0 0.0 copy-done.2
  380.0 2.3 convolution_bitcast_fusion
  382.3 0.0 reduce-scatter.2.cloned.1.call-update
  382.4 1.7 dynamic-slice_multiply_fusion
  384.0 65.7 %reduce-scatter.2.cloned.1.call-done = f32[8,64,128]{2,1,0:T(8,128)} async-done(((f32[8,64,1024]{2,1,0:T(8,128)}), f32[8,64,128]{2,1,0:T(8,128)}) %reduce-scatter.2.cloned.1.call-update) | async-done | bytes 262160 | tf_op jit(solution)/shard_map/reduce_scatter | solution.py:59
  449.7 1.7 broadcast_multiply_fusion
  (5 shorter events, 0.1 us)
Async XLA Ops:
  7.2 8.2 %copy-start = (bf16[8,64,1024]{2,1,0:T(8,128)(2,1)S(1)}, bf16[8,64,1024]{2,1,0:T(8,128)(2,1)}, u32[]{:S(2)}) copy-start(bf16[8,64,1024]{2,1,0:T(8,128)(2,1)} %param.13) | copy-start | bytes 3145732
  7.2 8.9 %copy-start.3 = (f32[2,64,64]{2,1,0:T(8,128)S(1)}, f32[2,64,64]{2,1,0:T(8,128)}, u32[]{:S(2)}) copy-start(f32[2,64,64]{2,1,0:T(8,128)} %param.12) | copy-start | bytes 98308
  7.2 10.6 %copy-start.5 = (s32[36,1]{0,1:T(1,128)S(1)}, s32[36,1]{0,1:T(1,128)}, u32[]{:S(2)}) copy-start(s32[36,1]{0,1:T(1,128)} %param.8) | copy-start | bytes 436
  7.2 254.2 %all-gather.3.cloned.1.call-start = ((), (), s32[]{:S(2)}) async-start(), calls=%async_computation.2 | async-start | bytes 18874368 | tf_op jit(solution)/shard_map/all_gather | solution.py:38
  15.4 0.7 copy-start.1
  18.8 3.8 copy-start.4
  32.7 417.0 %reduce-scatter.2.cloned.1.call-start = ((), (), s32[]{:S(2)}) async-start(), calls=%async_computation.1 | async-start | bytes 2359296 | tf_op jit(solution)/shard_map/reduce_scatter | solution.py:59
  377.4 2.6 copy-start.2
Sparse Core Ops, SparseCore 0:
  32.8 228.5 all-gather.2
  382.5 67.1 reduce-scatter.1
